TPU v7x, 256 devices: a whole 4x4x8 slice. The times are simulated.
256 devices in a mesh: row: 16 (over z, y_hi), col: 16 (over y_lo, x, core).
Axes of the slice: x: 4, y: 4 (y_hi: 2, y_lo: 2; y = y_hi * 2 + y_lo), z: 8, core: 2. Of those that a mesh axis runs over, the one named last changes fastest.
Arguments:
- covariance: float32 [12288, 12288], P('row', 'col'), may hold values from -6 to 6
- blocks: float32 [48, 5, 256, 256], P('col', None, 'row'), may hold values from -0.15625 to 0.15625
- present: int32 [48, 5], replicated, may hold values 0 or 1
- model_noise: float32 [12288, 12288], P('col', 'row'), may hold values from -6 to 6
Outputs:
- forecast: float32 [12288, 12288], P('col', 'row')
All inputs are finite; a program needn't handle non-finite values.
Results may differ from a plain program's by a relative error of at most 0.000057.
Values sent between devices are 32-bit elements; how exact they have to be, the bound alone decides.
A program may use at most 128 MiB of HBM per device.

v0:
```python
import jax
import jax.numpy as jnp
from jax import lax
from jax.sharding import PartitionSpec as P


def spread(array, axis, root):
    mine = lax.axis_index(axis) == root
    return lax.psum(jnp.where(mine, array, jnp.zeros_like(array)), axis)


def padded_2(cells, sides, width):
    for axis, dim in sides:
        count = lax.axis_size(axis)
        ends = count - 1
        head = lax.slice_in_dim(cells, 0, width, axis=dim)
        tail = lax.slice_in_dim(cells, cells.shape[dim] - width, cells.shape[dim], axis=dim)
        cells = jnp.concatenate(
            [
                lax.ppermute(tail, axis, [(i, (i + 1) % count) for i in range(ends)]),
                cells,
                lax.ppermute(head, axis, [((i + 1) % count, i) for i in range(ends)]),
            ],
            axis=dim,
        )
    return cells


def band_apply(live_band, padded):
    blocks_here = live_band.shape[0]
    block_size = live_band.shape[2]
    columns = padded.shape[1]
    summed = None
    for diagonal in range(5):
        window = padded[diagonal * block_size : (diagonal + blocks_here) * block_size].reshape(
            blocks_here, block_size, columns
        )
        term = jnp.einsum(
            "bij,bjw->biw",
            live_band[:, diagonal],
            window,
            precision=lax.Precision.HIGHEST,
            preferred_element_type=jnp.float32,
        )
        summed = term if summed is None else summed + term
    return summed.reshape(blocks_here * block_size, columns)


def banded(live_band, field, halo_fn):
    return band_apply(live_band, halo_fn(field))


def body(covariance, blocks, present, model_noise):
    row_index = lax.axis_index("row")
    col_index = lax.axis_index("col")
    ratio = lax.axis_size("row") // lax.axis_size("col")
    column_band = lax.all_gather(blocks, "row", axis=2, tiled=True)
    col_blocks = column_band.shape[0]
    row_blocks = col_blocks // ratio
    row_band = spread(column_band, "col", row_index // ratio)
    flags = present.astype(jnp.float32)
    col_flags = lax.dynamic_slice_in_dim(flags, col_index * col_blocks, col_blocks, 0)
    row_flags = lax.dynamic_slice_in_dim(flags, row_index * row_blocks, row_blocks, 0)
    live_col = column_band * col_flags[:, :, None, None]
    live_row = row_band * row_flags[:, :, None, None]
    margin = 2 * blocks.shape[3]

    def row_margin(field):
        return padded_2(field, (("row", 0),), margin)

    def col_margin(field):
        return padded_2(field, (("col", 0),), margin)

    mapped = banded(live_row, covariance, row_margin)
    second = banded(live_col, mapped.T, col_margin)
    return second + model_noise


def solution(mesh):
    in_specs = (P("row", "col"), P("col", None, "row", None), P(), P("col", "row"))
    out_specs = P("col", "row")
    return jax.shard_map(body, mesh=mesh, in_specs=in_specs, out_specs=out_specs, check_vma=False)
```

profile of v0, /device:TPU:8, one launch (start us, length us, event | category | flops | bytes accessed | tf_op | source)
XLA Modules:
  0.0 345.8 jit_solution(1013208820360126435)
XLA Ops:
  6.5 1.7 copy.5
  9.0 101.2 %all-gather.2.cloned.1.call-done = f32[3,5,256,256]{3,2,0,1:T(8,128)} async-done(((f32[3,5,16,256]{3,2,0,1:T(8,128)}), f32[3,5,256,256]{3,2,0,1:T(8,128)}) %all-gather.2.cloned.1.call-update) | async-done | bytes 3932176 | tf_op jit(solution)/shard_map/all_gather | solution.py:57
  110.2 6.0 %broadcast_multiply_fusion.1 = (f32[3,5,256,256]{3,2,0,1:T(8,128)}, f32[3,5,256,256]{3,2,0,1:T(8,128)}) fusion(f32[3,5,256,256]{3,2,0,1:T(8,128)} %all-gather.2.cloned.1.call-done, f32[3,5]{0,1:T(8,128)S(1)} %get-tuple-element.23, pred[]{:T(512)S(6)} %eq.3), kind=kLoop, calls=%fused_computation.13 | loop fusion | flops 1966080 | bytes 11796541 | tf_op jit(solution)/shard_map/mul | solution.py:64
  116.2 1.6 copy-done
  118.0 3.4 collective-permute-start
  122.8 82.2 %collective-permute-done = f32[512,768]{1,0:T(8,128)S(1)} collective-permute-done((f32[512,768]{1,0:T(8,128)S(1)}, f32[512,768]{1,0:T(8,128)S(1)}, u32[]{:S(2)}, u32[]{:S(2)}) %collective-permute-start) | collective-permute-done | bytes 1572896 | tf_op jit(solution)/shard_map/ppermute | solution.py:20
  205.6 2.6 fusion.11
  208.1 2.5 fusion.12
  210.7 45.9 %all-reduce.2.cloned.1.call-done = f32[3,5,256,256]{3,2,0,1:T(8,128)} async-done(((f32[3,5,256,256]{3,2,0,1:T(8,128)}), f32[3,5,256,256]{3,2,0,1:T(8,128)}) %all-reduce.2.cloned.1.call-update) | async-done | bytes 3932176 | tf_op jit(solution)/shard_map/psum | solution.py:9
  256.6 2.8 broadcast_multiply_fusion
  259.4 2.1 fusion.6
  261.6 2.1 fusion.8
  263.7 2.1 fusion.9
  265.8 2.1 fusion.7
  268.0 2.6 add_add_fusion.1
  270.6 2.2 fusion.13
  272.8 1.9 collective-permute-start.2
  274.7 5.8 %collective-permute-start.3 = (f32[512,768]{0,1:T(8,128)}, f32[512,768]{0,1:T(8,128)}, u32[]{:S(2)}, u32[]{:S(2)}) collective-permute-start(f32[512,768]{0,1:T(8,128)} %get-tuple-element.18), channel_id=1, source_target_pairs={{1,0},{2,1},{3,2},{4,3},{5,4},{6,5},{7,6},{8,7},{9,8},{10,9},{11,1... | collective-permute-start | bytes 4718600 | tf_op jit(solution)/shard_map/ppermute | solution.py:22
  280.5 2.0 copy.8
  282.4 5.4 %fusion.3 = f32[3,256,768]{2,1,0:T(8,128)} fusion(f32[3,256,768]{2,1,0:T(8,128)} %bitcast.63, f32[3,5,256,256]{3,2,0,1:T(8,128)} %get-tuple-element.9), kind=kOutput, calls=%fused_computation.18 | convolution fusion | flops 1811939328 | bytes 5505024 | tf_op jit(solution)/shard_map/bij,bjw->biw/dot_general | solution.py:38
  287.9 9.1 %collective-permute-done.2 = f32[512,768]{0,1:T(8,128)} collective-permute-done((f32[512,768]{0,1:T(8,128)}, f32[512,768]{0,1:T(8,128)}, u32[]{:S(2)}, u32[]{:S(2)}) %collective-permute-start.2) | collective-permute-done | bytes 1572896 | tf_op jit(solution)/shard_map/ppermute | solution.py:20
  297.0 1.8 collective-permute-done.3
  298.7 5.4 %pad_maximum_fusion = (f32[768,768]{0,1:T(8,128)}, f32[768,768]{0,1:T(8,128)}, f32[768,768]{0,1:T(8,128)}, f32[768,768]{0,1:T(8,128)}) fusion(f32[512,768]{0,1:T(8,128)} %collective-permute-done.3, f32[768,768]{0,1:T(8,128)S(1)} %bitcast.59, f32[512,768]{0,1:T(8,128)} %collective-permute-done.2), kind=kLoop, calls=%fused_computation.6 | loop fusion | flops 2359296 | bytes 14942208 | tf_op jit(solution)/shard_map/concatenate | solution.py:18
  304.1 3.1 copy.6
  307.2 5.6 %fusion.10 = f32[3,256,768]{2,1,0:T(8,128)} fusion(f32[3,256,768]{2,1,0:T(8,128)} %bitcast.64, f32[3,5,256,256]{3,2,0,1:T(8,128)} %get-tuple-element.9), kind=kOutput, calls=%fused_computation.32 | convolution fusion | flops 1811939328 | bytes 5505024 | tf_op jit(solution)/shard_map/bij,bjw->biw/dot_general | solution.py:38
  312.8 2.0 copy.7
  314.8 5.7 %fusion.4 = f32[3,256,768]{2,1,0:T(8,128)} fusion(f32[3,256,768]{2,1,0:T(8,128)} %bitcast.65, f32[3,5,256,256]{3,2,0,1:T(8,128)} %get-tuple-element.9), kind=kOutput, calls=%fused_computation.20 | convolution fusion | flops 1811939328 | bytes 5505024 | tf_op jit(solution)/shard_map/bij,bjw->biw/dot_general | solution.py:38
  320.4 2.0 copy.9
  322.4 5.6 %fusion.2 = f32[3,256,768]{2,1,0:T(8,128)} fusion(f32[3,256,768]{2,1,0:T(8,128)} %bitcast.66, f32[3,5,256,256]{3,2,0,1:T(8,128)} %get-tuple-element.9), kind=kOutput, calls=%fused_computation.16 | convolution fusion | flops 1811939328 | bytes 5505024 | tf_op jit(solution)/shard_map/bij,bjw->biw/dot_general | solution.py:38
  328.0 1.9 copy.10
  330.0 7.3 %add_add_fusion = f32[3,256,768]{2,1,0:T(8,128)S(1)} fusion(f32[3,256,768]{2,1,0:T(8,128)} %fusion.2, f32[3,256,768]{2,1,0:T(8,128)} %fusion.3, f32[3,256,768]{2,1,0:T(8,128)} %fusion.10, f32[3,256,768]{2,1,0:T(8,128)} %fusion.4, f32[3,256,768]{2,1,0:T(8,128)} %bitcast.61, f32[3,5,256,256]{3,2,0,1:T(8,128)} %get-tuple-element.9), kind=kOutput, calls=%fused_computation.9 | convolution fusion | flops 1814298624 | bytes 14942208 | tf_op jit(solution)/shard_map/bij,bjw->biw/dot_general | solution.py:38
  337.3 1.7 bitcast_add_fusion
  (29 shorter events, 3.0 us)
Async XLA Ops:
  6.5 103.7 %all-gather.2.cloned.1.call-start = ((), (), s32[]{:S(2)}) async-start(), calls=%async_computation | async-start | bytes 4177920 | tf_op jit(solution)/shard_map/all_gather | solution.py:57
  8.2 248.4 %all-reduce.2.cloned.1.call-start = ((), (), s32[]{:S(2)}) async-start(), calls=%async_computation.1 | async-start | bytes 7864320 | tf_op jit(solution)/shard_map/psum | solution.py:9
  116.2 1.7 copy-start
  118.0 86.9 %collective-permute-start = (f32[512,768]{1,0:T(8,128)S(1)}, f32[512,768]{1,0:T(8,128)S(1)}, u32[]{:S(2)}, u32[]{:S(2)}) collective-permute-start(f32[512,768]{1,0:T(8,128)S(1)} %get-tuple-element.21), channel_id=1, source_target_pairs={{0,16},{16,32},{32,48},{48,64},{64,80},{80,96},{96,112},{112,128},... | collective-permute-start | bytes 4718600 | tf_op jit(solution)/shard_map/ppermute | solution.py:20
  121.5 84.0 %collective-permute-start.1 = (f32[512,768]{1,0:T(8,128)S(1)}, f32[512,768]{1,0:T(8,128)S(1)}, u32[]{:S(2)}, u32[]{:S(2)}) collective-permute-start(f32[512,768]{1,0:T(8,128)S(1)} %get-tuple-element.22), channel_id=1, source_target_pairs={{16,0},{32,16},{48,32},{64,48},{80,64},{96,80},{112,96},{128,112},... | collective-permute-start | bytes 4718600 | tf_op jit(solution)/shard_map/ppermute | solution.py:22
  256.6 2.8 copy-start.5
  259.4 2.1 copy-start.7
  261.6 2.1 copy-start.6
  265.8 2.1 copy-start.4
  272.8 24.1 %collective-permute-start.2 = (f32[512,768]{0,1:T(8,128)}, f32[512,768]{0,1:T(8,128)}, u32[]{:S(2)}, u32[]{:S(2)}) collective-permute-start(f32[512,768]{0,1:T(8,128)} %get-tuple-element.17), channel_id=1, source_target_pairs={{0,1},{1,2},{2,3},{3,4},{4,5},{5,6},{6,7},{7,8},{8,9},{9,10},{10,1... | collective-permute-start | bytes 4718600 | tf_op jit(solution)/shard_map/ppermute | solution.py:20
  274.7 24.0 %collective-permute-start.3 = (f32[512,768]{0,1:T(8,128)}, f32[512,768]{0,1:T(8,128)}, u32[]{:S(2)}, u32[]{:S(2)}) collective-permute-start(f32[512,768]{0,1:T(8,128)} %get-tuple-element.18), channel_id=1, source_target_pairs={{1,0},{2,1},{3,2},{4,3},{5,4},{6,5},{7,6},{8,7},{9,8},{10,9},{11,1... | collective-permute-start | bytes 4718600 | tf_op jit(solution)/shard_map/ppermute | solution.py:22
  307.2 5.6 %copy-start.3 = (f32[768,768]{0,1:T(8,128)S(1)}, f32[768,768]{0,1:T(8,128)}, u32[]{:S(2)}) copy-start(f32[768,768]{0,1:T(8,128)} %get-tuple-element.16) | copy-start | bytes 7077892
  314.8 5.7 %copy-start.2 = (f32[768,768]{0,1:T(8,128)S(1)}, f32[768,768]{0,1:T(8,128)}, u32[]{:S(2)}) copy-start(f32[768,768]{0,1:T(8,128)} %get-tuple-element.6) | copy-start | bytes 7077892
  322.4 5.6 %copy-start.1 = (f32[768,768]{0,1:T(8,128)S(1)}, f32[768,768]{0,1:T(8,128)}, u32[]{:S(2)}) copy-start(f32[768,768]{0,1:T(8,128)} %get-tuple-element.5) | copy-start | bytes 7077892
  330.0 7.3 %copy-start.8 = (f32[768,768]{1,0:T(8,128)S(1)}, f32[768,768]{1,0:T(8,128)}, u32[]{:S(2)}) copy-start(f32[768,768]{1,0:T(8,128)} %param.7) | copy-start | bytes 7077892
Sparse Core Ops, SparseCore 0:
  9.9 100.2 all-gather.1
  116.3 140.2 all-reduce.1
where the time goes:
time: 348 us; the launch traced here: 346 us
  waiting for transfers between devices  240 us (69%)
  matrix products  40.7 us (12%)
  local copies, waits for them, and re-layouts  22.4 us (6%)
  other arithmetic  16.5 us (5%)
  between operations  13.6 us (4%)
  starting transfers between devices  12.4 us (4%)
    all_gather x1, waiting for transfers between devices, body(): column_band = lax.all_gather(blocks, 'row', axis=2, tiled=True)  101 us
    ppermute x2, waiting for transfers between devices, padded_2(): lax.ppermute(tail, axis, [(i, (i + 1) % count) for i in range(ends)])  91.3 us
    psum x1, waiting for transfers between devices, spread(): return lax.psum(jnp.where(mine, array, jnp.zeros_like(array)), axis)  45.9 us
    dot_general x10, matrix products, band_apply(): jnp.einsum('bij,bjw->biw', live_band[:, diagonal], window, precision=lax....  40.7 us
    slice x6, local copies, waits for them, and re-layouts, band_apply(): padded[diagonal * block_size:(diagonal + blocks_here) * block_size]  14 us
    ppermute x2, starting transfers between devices, padded_2(): lax.ppermute(head, axis, [((i + 1) % count, i) for i in range(ends)])  7.04 us
  transfers between devices with their start and end apart: 6, of which 5 were waited for; matrix products, arithmetic and copies ran while one was open for 4% of the time, Pallas kernels for 0%

commit v1 on v0

v1 whole, which is shorter than its diff:
```python
import functools

import jax
import jax.numpy as jnp
from jax import lax
from jax.experimental import pallas as pl
from jax.experimental.pallas import tpu as pltpu
from jax.sharding import PartitionSpec as P

MESH = pl.DeviceIdType.MESH
F32 = jnp.float32
BF16 = jnp.bfloat16
CHUNKS = 6
WIDE = 128
ORDER = (0, 1, 4, 5, 2, 3)


def split(value):
    high = value.astype(BF16)
    return high, (value - high.astype(F32)).astype(BF16)


def kernel(p_hbm, blk_hbm, pres, q_hbm, out_hbm, win, edge, mrow, mcol, mrow_b, mcol_b, win_b, mapped, halo, bhi, blo, total, ssem, rsem, lsem):
    r = lax.axis_index("row")
    c = lax.axis_index("col")
    z, yh = r // 2, r % 2
    g, k = c // 2, c % 2
    yl, x = g // 4, g % 4

    def at_z(step):
        return ((r + 2 * step + 32) % 16, c)

    def at_x(step):
        return (r, yl * 8 + ((x + step + 4) % 4) * 2 + k)

    partner = (r + 1 - 2 * yh, c)
    mate = (r, c + 1 - 2 * k)
    twin = (r, (c + 8) % 16)
    left = (r, (c + 15) % 16)
    right = (r, (c + 1) % 16)
    turn = lambda n: n + 4 * ((8 - n) // 8)
    there = (c, 2 * ((turn(g) + z) % 8) + yh)
    source_z = (g - turn(z) + 8) % 8
    origin = (2 * source_z + k, r)

    ids = {}

    def ident(name):
        return ids.setdefault(name, len(ids))

    sent = []

    def send(name, src, dst, device):
        n = ident(name)
        copy = pltpu.make_async_remote_copy(src, dst, ssem.at[n], rsem.at[n], device_id=device, device_id_type=MESH)
        copy.start()
        sent.append(copy)

    def arrived(name, dst):
        n = ident(name)
        pltpu.make_async_remote_copy(dst, dst, ssem.at[n], rsem.at[n], device_id=mate, device_id_type=MESH).wait_recv()

    lids = {}

    def local(name, src, dst):
        n = lids.setdefault(name, len(lids))
        copy = pltpu.make_async_copy(src, dst, lsem.at[n])
        copy.start()
        return copy

    def cols(q):
        return pl.ds(q * WIDE, WIDE)

    barrier = pltpu.get_barrier_semaphore()
    peers = (partner, at_z(1), at_z(-1), mate, twin, at_x(1), at_x(-1), at_x(2), left, right, there, origin)
    for peer in peers:
        pl.semaphore_signal(barrier, inc=1, device_id=peer, device_id_type=MESH)
    pl.semaphore_wait(barrier, len(peers))

    slot = k * 8 + x * 2 + yl
    pair = k * 8 + x * 2

    def send_blocks():
        send("col_y", blk_hbm, mcol.at[r], partner)
        g2 = (turn(g) + z) % 8
        send("row_t", blk_hbm, mrow.at[yh * 8 + (g2 % 4) * 2 + g2 // 4], there)

    def send_direct(q):
        send(f"direct{q}", p_hbm.at[pl.ds(256 * (1 - yh), 512), cols(q)], win.at[q, pl.ds(1280 * yh, 512)], partner)

    def send_edge(q):
        send(f"edge{q}", p_hbm.at[pl.ds(512 * yh, 256), cols(q)], edge.at[q], at_z(2 * yh - 1))

    def relay_edge(q):
        arrived(f"edge{q}", edge.at[q])
        send(f"cross{q}", edge.at[q], win.at[q, pl.ds(256 * (5 - 4 * yh), 256)], partner)

    def relay_middle(q):
        arrived(f"direct{q}", win.at[q, pl.ds(0, 512)])
        send(f"middle{q}", win.at[q, pl.ds(1536 * (1 - yh), 256)], win.at[q, pl.ds(1536 * yh, 256)], at_z(1 - 2 * yh))

    major = 1 - 2 * k

    def zpair(n):
        return pl.ds(2 * ((n + 16) % 8), 2)

    def ring_first():
        arrived("col_y", mcol.at[r])
        for name, sign in (("major0", 1), ("minor0", -1)):
            send(name, mcol.at[zpair(z)], mcol.at[zpair(z)], at_z(sign * major))

    def ring_major(t):
        who = zpair(z - major * t)
        arrived(f"major{t - 1}", mcol.at[who])
        if t < 4:
            send(f"major{t}", mcol.at[who], mcol.at[who], at_z(major))

    def ring_minor(t):
        who = zpair(z + major * t)
        arrived(f"minor{t - 1}", mcol.at[who])
        if t < 3:
            send(f"minor{t}", mcol.at[who], mcol.at[who], at_z(-major))

    def row_twin():
        arrived("row_t", mrow.at[slot])
        send("row_y", mrow.at[slot], mrow.at[slot], twin)

    def row_spread():
        arrived("row_y", mrow.at[slot])
        mine = mrow.at[pl.ds(pair, 2)]
        for step in (1, -1, 2):
            send(f"row_x{step}", mine, mine, at_x(step))
        send("row_m0", mine, mine, mate)

    def row_mate(step):
        who = mrow.at[pl.ds(k * 8 + ((x - step + 4) % 4) * 2, 2)]
        arrived(f"row_x{step}", who)
        send(f"row_m{step}", who, who, mate)

    def row_done():
        for step in (0, 1, -1, 2):
            arrived(f"row_m{step}", mrow.at[pl.ds(pair, 2)])

    def flag(b, d, first):
        at = first + b
        inside = at + d - 2
        good = ((inside + 48) // 48) * ((95 - inside) // 48)
        good = good - (good // 2) * good
        return (pres[at, d] * good).astype(F32)

    def convert(src, dst, first, place):
        flags = [[flag(b, d, first) for d in range(5)] for b in range(3)]

        @pl.loop(0, 16)
        def _(s):
            row = place(s)
            for b in range(3):
                for d in range(5):
                    high, low = split(src[s, b, d] * flags[b][d])
                    dst[b, pl.ds(pl.multiple_of(row * 16, 16), 16), d * 256 : (d + 1) * 256] = high
                    dst[b, pl.ds(pl.multiple_of(256 + row * 16, 16), 16), d * 256 : (d + 1) * 256] = low

    def row_place(s):
        g2 = 4 * (s % 2) + (s % 8) // 2
        return 2 * ((g2 - turn(z) + 8) % 8) + s // 8

    def stage_one(q):
        arrived(f"cross{q}", edge.at[q])
        arrived(f"middle{q}", edge.at[q])

        @pl.loop(0, 7)
        def _(t):
            rows = pl.ds(pl.multiple_of(t * 256, 256), 256)
            high, low = split(win[q, rows])
            win_b[rows, 0:WIDE] = high
            win_b[rows, WIDE : 2 * WIDE] = low

        @pl.loop(0, 3)
        def _(i):
            rows = pl.ds(pl.multiple_of(i * 256, 256), 256)
            part = jnp.dot(mrow_b[i], win_b[pl.ds(pl.multiple_of(i * 256, 256), 1280), :], preferred_element_type=F32)
            part = part[:256] + part[256:]
            part = part[:, :WIDE] + part[:, WIDE:]
            mapped[q, rows] = part
            high, low = split(part)
            bhi[rows, 512 + q * WIDE : 512 + (q + 1) * WIDE] = high
            blo[rows, 512 + q * WIDE : 512 + (q + 1) * WIDE] = low

        if q < 4:
            send(f"left{q}", mapped.at[q], halo.at[4 + q], left)
        if q > 1:
            send(f"right{q}", mapped.at[q], halo.at[q - 2], right)

    def take_halo(n):
        if n < 4:
            arrived(f"right{n + 2}", halo.at[n])
            base = n * WIDE
        else:
            arrived(f"left{n - 4}", halo.at[n])
            base = 1280 + (n - 4) * WIDE

        @pl.loop(0, 3)
        def _(i):
            rows = pl.ds(pl.multiple_of(i * 256, 256), 256)
            high, low = split(halo[n, rows])
            bhi[rows, base : base + WIDE] = high
            blo[rows, base : base + WIDE] = low

    def product(i, spot, count):
        d = spot - i
        depth = count * 256
        a = mcol_b[i, :, d * 256 : d * 256 + depth]
        rows = slice(i * 256, (i + 1) * 256)
        dims = (((1,), (1,)), ((), ()))

        @pl.loop(0, 3)
        def _(n):
            these = pl.ds(pl.multiple_of(n * 256, 256), 256)
            one = lax.dot_general(a, bhi[these, spot * 256 : spot * 256 + depth], dims, preferred_element_type=F32)
            two = lax.dot_general(a[:256], blo[these, spot * 256 : spot * 256 + depth], dims, preferred_element_type=F32)
            place = pl.ds(pl.multiple_of(n * 256, 256), 256)
            total[rows, place] += one[:256] + one[256:] + two

    own_blocks = local("blk", blk_hbm, mcol.at[r])
    send_blocks()
    send_direct(ORDER[0])
    send_edge(ORDER[0])
    send_edge(ORDER[1])
    own = [local(f"own{q}", p_hbm.at[:, cols(q)], win.at[q, pl.ds(512, 768)]) for q in ORDER]
    noise = local("noise", q_hbm, total)
    send_direct(ORDER[1])
    relay_edge(ORDER[0])
    own_blocks.wait()
    ring_first()
    for q in ORDER[2:]:
        send_edge(q)
    send_direct(ORDER[2])
    row_twin()
    relay_middle(ORDER[0])
    relay_edge(ORDER[1])
    send_direct(ORDER[3])
    row_spread()
    relay_middle(ORDER[1])
    relay_edge(ORDER[2])
    ring_major(1)
    ring_minor(1)
    send_direct(ORDER[4])
    relay_edge(ORDER[3])
    relay_middle(ORDER[2])
    row_mate(1)
    row_mate(-1)
    send_direct(ORDER[5])
    relay_edge(ORDER[4])
    relay_middle(ORDER[3])
    ring_major(2)
    ring_minor(2)
    row_mate(2)
    relay_edge(ORDER[5])
    relay_middle(ORDER[4])
    row_done()
    convert(mrow, mrow_b, 3 * r, row_place)
    for copy in own:
        copy.wait()
    stage_one(ORDER[0])
    relay_middle(ORDER[5])
    ring_major(3)
    stage_one(ORDER[1])
    ring_minor(3)
    stage_one(ORDER[2])
    stage_one(ORDER[3])
    ring_major(4)
    convert(mcol, mcol_b, 3 * c, lambda s: s)
    noise.wait()
    stage_one(ORDER[4])
    stage_one(ORDER[5])
    for n in (4, 5, 2, 3):
        take_halo(n)
    product(0, 1, 2)
    product(0, 4, 1)
    product(1, 1, 2)
    product(1, 4, 2)
    product(2, 2, 1)
    product(2, 4, 2)
    for n in (0, 1, 6, 7):
        take_halo(n)
    product(0, 0, 1)
    product(0, 3, 1)
    outs = [local("out0", total.at[0:256], out_hbm.at[0:256])]
    product(1, 3, 1)
    outs.append(local("out1", total.at[256:512], out_hbm.at[256:512]))
    product(2, 3, 1)
    product(2, 6, 1)
    outs.append(local("out2", total.at[512:768], out_hbm.at[512:768]))
    for copy in sent:
        copy.wait_send()
    for copy in outs:
        copy.wait()


def body(covariance, blocks, present, model_noise):
    anywhere = pl.BlockSpec(memory_space=pl.ANY)
    return pl.pallas_call(
        kernel,
        out_shape=jax.ShapeDtypeStruct((768, 768), F32),
        in_specs=[anywhere, anywhere, pl.BlockSpec(memory_space=pltpu.SMEM), anywhere],
        out_specs=anywhere,
        scratch_shapes=[
            pltpu.VMEM((CHUNKS, 1792, WIDE), F32),
            pltpu.VMEM((CHUNKS, 256, WIDE), F32),
            pltpu.VMEM((16, 3, 5, 16, 256), F32),
            pltpu.VMEM((16, 3, 5, 16, 256), F32),
            pltpu.VMEM((3, 512, 1280), BF16),
            pltpu.VMEM((3, 512, 1280), BF16),
            pltpu.VMEM((1792, 2 * WIDE), BF16),
            pltpu.VMEM((CHUNKS, 768, WIDE), F32),
            pltpu.VMEM((8, 768, WIDE), F32),
            pltpu.VMEM((768, 1792), BF16),
            pltpu.VMEM((768, 1792), BF16),
            pltpu.VMEM((768, 768), F32),
            pltpu.SemaphoreType.DMA((64,)),
            pltpu.SemaphoreType.DMA((64,)),
            pltpu.SemaphoreType.DMA((16,)),
        ],
        compiler_params=pltpu.CompilerParams(collective_id=0, has_side_effects=True, vmem_limit_bytes=60 << 20),
        name="forecast",
    )(covariance, blocks, present, model_noise)


def solution(mesh):
    in_specs = (P("row", "col"), P("col", None, "row", None), P(), P("col", "row"))
    out_specs = P("col", "row")
    return jax.shard_map(body, mesh=mesh, in_specs=in_specs, out_specs=out_specs, check_vma=False)
```

time: 348 us -> 125 us (0.36)
  the two profiles are of different devices: /device:TPU:8 before, /device:TPU:121 now
where the time goes in v1:
time: 125 us
  Pallas kernels  120 us (96%)
  local copies, waits for them, and re-layouts  4.6 us (4%)
    pallas_call x1, Pallas kernels, body(): pl.pallas_call(kernel, out_shape=jax.ShapeDtypeStruct((768, 768), F32), i...  120 us
    unnamed x2, local copies, waits for them, and re-layouts  4.6 us

profile of v1, /device:TPU:121, one launch (start us, length us, event | category | flops | bytes accessed | tf_op | source)
XLA Modules:
  0.0 124.8 jit_solution(6705208882587858212)
XLA Ops:
  0.0 1.4 %copy.5.pres = s32[48,5]{1,0:T(8,128)} copy(s32[48,5]{0,1:T(8,128)} %param.6) | data formatting | bytes 1920 | tf_op args[2]
  1.4 120.2 %forecast.1 = f32[768,768]{1,0:T(8,128)} custom-call(f32[768,768]{1,0:T(8,128)} %p_hbm.1, f32[3,5,16,256]{3,2,1,0:T(8,128)} %blk_hbm.1, s32[48,5]{1,0:T(8,128)} %copy.5.pres, f32[768,768]{1,0:T(8,128)} %q_hbm.1), custom_call_target="tpu_custom_call" | custom-call | tf_op jit(solution)/shard_map/forecast/pallas_call | solution.py:302
  121.6 3.2 %copy.7 = f32[768,768]{1,0:T(8,128)} copy(f32[768,768]{1,0:T(8,128)} %forecast.1) | data formatting | bytes 4718592

commit v2 on v1

v2 whole, which is shorter than its diff:
```python
import functools

import jax
import jax.numpy as jnp
from jax import lax
from jax.experimental import pallas as pl
from jax.experimental.pallas import tpu as pltpu
from jax.sharding import PartitionSpec as P

MESH = pl.DeviceIdType.MESH
F32 = jnp.float32
BF16 = jnp.bfloat16
CHUNKS = 6
PARTS = 4
SEAM = 7
WIDE = 128
ORDER = (0, 1, 4, 5, 2, 3)

SCHEDULE = (
    ("col_y",), ("t1", 0), ("t1", 1), ("t1", 2), ("direct", 0), ("edge", 2), ("ring", 0), ("edge", 0),
    ("edge", 1), ("direct", 1), ("t2", 0), ("t2", 1), ("minor", 0, 1), ("t2", 2), ("major", 0, 1),
    ("cross", 0), ("ring", 1), ("cross", 1), ("direct", 2), ("middle", 0), ("edge", 3), ("ty", 0), ("ty", 1),
    ("major", 0, 2), ("minor", 0, 2), ("ty", 2), ("cross", 2), ("middle", 1), ("direct", 3), ("tx", 0),
    ("major", 1, 1), ("minor", 1, 1), ("middle", 2), ("edge", 4), ("tx", 1), ("tx", 2), ("tf", 0),
    ("cross", 3), ("major", 0, 3), ("minor", 0, 3), ("tf", 1), ("direct", 4), ("tf", 2), ("edge", 5),
    ("major", 1, 2), ("minor", 1, 2), ("tm", 1), ("tm", 0), ("tm", 2), ("cross", 4), ("middle", 3),
    ("direct", 5), ("tc", 0), ("tc", 1), ("tc", 2), ("one", 0), ("major", 0, 4), ("one", 1), ("hop", 0),
    ("major", 1, 3), ("minor", 1, 3), ("cross", 5), ("one", 2), ("hop", 1), ("hop", 2), ("middle", 4),
    ("one", 3), ("major", 1, 4), ("cc",), ("noise",), ("middle", 5), ("hop", 3), ("one", 4), ("take", 4),
    ("take", 5), ("take", 2), ("take", 3), ("prod", 0, 1, 2), ("prod", 0, 4, 1), ("prod", 1, 1, 2), ("hop", 4),
    ("one", 5), ("prod", 1, 4, 2), ("prod", 2, 2, 1), ("prod", 2, 4, 2), ("prod", 0, 3, 1), ("prod", 1, 3, 1),
    ("out", 1), ("hop", 5), ("prod", 2, 3, 1), ("take", 0), ("take", 1), ("prod", 0, 0, 1), ("out", 0),
    ("take", 6), ("take", 7), ("prod", 2, 6, 1), ("out", 2),
)


def split(value):
    high = value.astype(BF16)
    return high, (value - high.astype(F32)).astype(BF16)


def kernel(p_hbm, blk_hbm, pres_hbm, q_hbm, out_hbm, win, edge, hop, detour, mrow, mcol, mrow_b, mcol_b, win_b, mapped, halo, bhi, blo, total, pres, ssem, rsem, lsem):
    r = lax.axis_index("row")
    c = lax.axis_index("col")
    z, yh = r // 2, r % 2
    g, k = c // 2, c % 2
    yl, x = g // 4, g % 4

    def at_z(step):
        return ((r + 2 * step + 32) % 16, c)

    def at_x(step, core):
        return (r, yl * 8 + ((x + step + 8) % 4) * 2 + core)

    partner = (r + 1 - 2 * yh, c)
    mate = (r, c + 1 - 2 * k)
    twin = (r, (c + 8) % 16)
    left = (r, (c + 15) % 16)
    right = (r, (c + 1) % 16)
    first_to, first_from = at_x(z, 1 - k), at_x(-z, 1 - k)
    k0 = 1 - k
    yl_to = (yl + yh + k0) % 2
    core_to = (z // 4 + yl + k0) % 2
    second_to = (2 * (4 * yl + (x - z + 8) % 4) + k0, yl_to * 8 + x * 2 + core_to)

    def held(core, xs, ys):
        return (xs - z % 4 + 4) % 4 + 4 * ((core + z // 4 + yh) % 2), (yh + ys + z // 4) % 2

    z_from, yh_from = held(k, x, yl)
    second_from = (2 * z_from + yh_from, (z // 4) * 8 + x * 2 + 1 - yh)

    ids = {}

    def ident(name):
        return ids.setdefault(name, len(ids))

    def part_rows(part):
        return pl.ds(part * (768 // PARTS), 768 // PARTS)

    sent = []

    def send(name, src, dst, device, when=None):
        n = ident(name)
        copy = pltpu.make_async_remote_copy(src, dst, ssem.at[n], rsem.at[n], device_id=device, device_id_type=MESH)
        if when is None:
            copy.start()
        else:
            pl.when(when)(copy.start)
        sent.append((copy, when))

    def arrived(name, dst):
        n = ident(name)
        pltpu.make_async_remote_copy(dst, dst, ssem.at[n], rsem.at[n], device_id=mate, device_id_type=MESH).wait_recv()

    lids = {}

    def local(name, src, dst):
        n = lids.setdefault(name, len(lids))
        copy = pltpu.make_async_copy(src, dst, lsem.at[n])
        copy.start()
        return copy

    def cols(q):
        return pl.ds(q * WIDE, WIDE)

    own_flags = local("flags", pres_hbm, pres)
    own_blocks = local("blk", blk_hbm, mcol.at[r])
    own = [local(f"own{q}", p_hbm.at[:, cols(q)], win.at[q, pl.ds(512, 768)]) for q in ORDER]
    noise = local("noise", q_hbm, total)

    barrier = pltpu.get_barrier_semaphore()
    peers = (partner, at_z(1), at_z(-1), mate, twin, at_x(1, k), at_x(-1, k), left, right, first_to, first_from, second_to, second_from)
    for peer in peers:
        pl.semaphore_signal(barrier, inc=1, device_id=peer, device_id_type=MESH)
    seam = (c == SEAM) | (c == SEAM + 1)
    helps_right = (yl == 1) & (k == 0) & (x > 0)
    helps_left = (yl == 0) & (k == 1) & (x < 3)
    helps = helps_right | helps_left

    def greet(columns):
        for column in columns:
            pl.semaphore_signal(barrier, inc=1, device_id=(r, column), device_id_type=MESH)

    pl.when(seam)(lambda: greet((1, 3, 5, 10, 12, 14)))
    pl.when(helps)(lambda: greet((SEAM, SEAM + 1)))
    plain = jnp.logical_not(seam | helps)
    pl.when(plain)(lambda: pl.semaphore_wait(barrier, len(peers)))
    pl.when(seam)(lambda: pl.semaphore_wait(barrier, len(peers) + 6))
    pl.when(helps & jnp.logical_not(seam))(lambda: pl.semaphore_wait(barrier, len(peers) + 2))

    slot = k * 8 + x * 2 + yl

    def slot_of(step):
        return k * 8 + ((x + step + 4) % 4) * 2

    def col_y():
        send("col_y", blk_hbm, mcol.at[r], partner)

    def direct(q):
        send(f"direct{q}", p_hbm.at[pl.ds(256 * (1 - yh), 512), cols(q)], win.at[q, pl.ds(1280 * yh, 512)], partner)

    def edge_(q):
        send(f"edge{q}", p_hbm.at[pl.ds(512 * yh, 256), cols(q)], edge.at[q], at_z(2 * yh - 1))

    def cross(q):
        arrived(f"edge{q}", edge.at[q])
        send(f"cross{q}", edge.at[q], win.at[q, pl.ds(256 * (5 - 4 * yh), 256)], partner)

    def middle(q):
        arrived(f"direct{q}", win.at[q, pl.ds(0, 512)])
        send(f"middle{q}", win.at[q, pl.ds(1536 * (1 - yh), 256)], win.at[q, pl.ds(1536 * yh, 256)], at_z(1 - 2 * yh))

    major = 1 - 2 * k

    def level(step, other):
        return 2 * ((z + step + 16) % 8) + (1 - yh if other else yh)

    def ring(other):
        if other:
            arrived("col_y", mcol.at[level(0, 1)])
        src = mcol.at[level(0, 1)] if other else blk_hbm
        for tag, sign in (("major", 1), ("minor", -1)):
            send(f"{tag}{other}_0", src, mcol.at[level(0, other)], at_z(sign * major))

    def major_(other, t):
        who = mcol.at[level(-major * t, other)]
        arrived(f"major{other}_{t - 1}", who)
        if t < 4:
            send(f"major{other}_{t}", who, who, at_z(major))

    def minor_(other, t):
        who = mcol.at[level(major * t, other)]
        arrived(f"minor{other}_{t - 1}", who)
        if t < 3:
            send(f"minor{other}_{t}", who, who, at_z(-major))

    def t1(b):
        send(f"row_a{b}", blk_hbm.at[b], hop.at[b], first_to)

    def t2(b):
        arrived(f"row_a{b}", hop.at[b])
        send(f"row_b{b}", hop.at[b], mrow.at[core_to * 8 + x * 2 + yl_to, b], second_to)

    def ty(b):
        arrived(f"row_b{b}", mrow.at[slot, b])
        send(f"row_y{b}", mrow.at[slot, b], mrow.at[slot, b], twin)

    def pair_at(step, b):
        return mrow.at[pl.ds(slot_of(step), 2), b]

    def tx(b):
        arrived(f"row_y{b}", mrow.at[slot, b])
        mine = pair_at(0, b)
        send(f"row_p{b}", mine, mine, at_x(1, k))
        send(f"row_n{b}", mine, mine, at_x(-1, k))
        send(f"row_m0{b}", mine, mine, mate)

    def tf(b):
        for tag, step, half in (("p", -1, 0), ("n", 1, 1)):
            arrived(f"row_{tag}{b}", pair_at(step, b))
            one = mrow.at[slot_of(step) + half, b]
            send(f"row_{tag}{tag}{b}", one, one, at_x(-step, k))
            send(f"row_m{tag}{b}", pair_at(step, b), pair_at(step, b), mate)

    def tm(b):
        for tag, half in (("p", 0), ("n", 1)):
            one = mrow.at[slot_of(2) + half, b]
            arrived(f"row_{tag}{tag}{b}", one)
            send(f"row_m{tag}{tag}{b}", one, one, mate)

    def td(b):
        for name in ("m0", "mp", "mn"):
            arrived(f"row_{name}{b}", pair_at(0, b))
        for name in ("mpp", "mnn"):
            arrived(f"row_{name}{b}", mrow.at[slot, b])

    def flag(b, d, first):
        at = first + b
        inside = at + d - 2
        good = ((inside + 48) // 48) * ((95 - inside) // 48)
        return (pres[at, d] * good).astype(F32)

    def convert(src, dst, first, place, b):
        flags = [flag(b, d, first) for d in range(5)]

        @pl.loop(0, 16)
        def _(s):
            row = place(s)
            for d in range(5):
                high, low = split(src[s, b, d] * flags[d])
                dst[b, pl.ds(pl.multiple_of(row * 16, 16), 16), d * 256 : (d + 1) * 256] = high
                dst[b, pl.ds(pl.multiple_of(256 + row * 16, 16), 16), d * 256 : (d + 1) * 256] = low

    def row_place(s):
        zs, ys = held(s // 8, (s % 8) // 2, s % 2)
        return 2 * zs + ys

    def tc(b):
        td(b)
        if b == 0:
            own_flags.wait()
        convert(mrow, mrow_b, 3 * r, row_place, b)

    def cc():
        own_blocks.wait()
        for b in range(3):
            convert(mcol, mcol_b, 3 * c, lambda s: s, b)

    def pass_on(side, q, n, when, target, base):
        send(f"{side}_part{q}_0", mapped.at[q, part_rows(0)], halo.at[n, part_rows(0)], (r, target), when)
        for part in range(1, PARTS):
            send(f"{side}_hop{q}_{part}", mapped.at[q, part_rows(part)], detour.at[q], (r, base + 2 * part), when)

    def relay(side, q, n, when, target, part):
        @pl.when(when)
        def _():
            for number in range(1, PARTS):
                @pl.when(part == number)
                def _():
                    arrived(f"{side}_hop{q}_{number}", detour.at[q])
        for number in range(1, PARTS):
            send(f"{side}_part{q}_{number}", detour.at[q], halo.at[n, part_rows(number)], (r, target), when & (part == number))

    def hop_(q):
        if q < 4:
            relay("left", q, 4 + q, helps_left, SEAM, x + 1)
        if q > 1:
            relay("right", q, q - 2, helps_right, SEAM + 1, x)

    def one(q):
        own[ORDER.index(q)].wait()
        arrived(f"cross{q}", edge.at[q])
        arrived(f"middle{q}", edge.at[q])

        @pl.loop(0, 7)
        def _(t):
            rows = pl.ds(pl.multiple_of(t * 256, 256), 256)
            high, low = split(win[q, rows])
            win_b[rows, 0:WIDE] = high
            win_b[rows, WIDE : 2 * WIDE] = low

        @pl.loop(0, 3)
        def _(i):
            rows = pl.ds(pl.multiple_of(i * 256, 256), 256)
            part = jnp.dot(mrow_b[i], win_b[pl.ds(pl.multiple_of(i * 256, 256), 1280), :], preferred_element_type=F32)
            part = part[:256] + part[256:]
            part = part[:, :WIDE] + part[:, WIDE:]
            mapped[q, rows] = part
            high, low = split(part)
            bhi[rows, 512 + q * WIDE : 512 + (q + 1) * WIDE] = high
            blo[rows, 512 + q * WIDE : 512 + (q + 1) * WIDE] = low

        if q < 4:
            send(f"left{q}", mapped.at[q], halo.at[4 + q], left, (c > 0) & (c != SEAM + 1))
            pass_on("left", q, 4 + q, c == SEAM + 1, SEAM, -1)
        if q > 1:
            send(f"right{q}", mapped.at[q], halo.at[q - 2], right, (c < 15) & (c != SEAM))
            pass_on("right", q, q - 2, c == SEAM, SEAM + 1, 8)

    def take(n):
        if n < 4:
            name, base, there = f"right{n + 2}", n * WIDE, c > 0
        else:
            name, base, there = f"left{n - 4}", 1280 + (n - 4) * WIDE, c < 15

        @pl.when(there)
        def _():
            split_up = c == (SEAM + 1 if n < 4 else SEAM)
            pl.when(jnp.logical_not(split_up))(lambda: arrived(name, halo.at[n]))

            @pl.when(split_up)
            def _():
                for part in range(PARTS):
                    arrived(f"{name[:-1]}_part{name[-1]}_{part}", halo.at[n, part_rows(part)])

            @pl.loop(0, 3)
            def _(i):
                rows = pl.ds(pl.multiple_of(i * 256, 256), 256)
                high, low = split(halo[n, rows])
                bhi[rows, base : base + WIDE] = high
                blo[rows, base : base + WIDE] = low

        @pl.when(jnp.logical_not(there))
        def _():
            bhi[:, base : base + WIDE] = jnp.zeros((768, WIDE), BF16)
            blo[:, base : base + WIDE] = jnp.zeros((768, WIDE), BF16)

    def prod(i, spot, count):
        d = spot - i
        depth = count * 256
        a = mcol_b[i, :, d * 256 : d * 256 + depth]
        rows = slice(i * 256, (i + 1) * 256)
        dims = (((1,), (1,)), ((), ()))

        @pl.loop(0, 3)
        def _(n):
            these = pl.ds(pl.multiple_of(n * 256, 256), 256)
            first = lax.dot_general(a, bhi[these, spot * 256 : spot * 256 + depth], dims, preferred_element_type=F32)
            second = lax.dot_general(a[:256], blo[these, spot * 256 : spot * 256 + depth], dims, preferred_element_type=F32)
            total[rows, these] += first[:256] + first[256:] + second

    outs = []

    def out(i):
        outs.append(local(f"out{i}", total.at[i * 256 : (i + 1) * 256], out_hbm.at[i * 256 : (i + 1) * 256]))

    actions = dict(col_y=col_y, direct=direct, edge=edge_, cross=cross, middle=middle, ring=ring, major=major_, minor=minor_, t1=t1, t2=t2, ty=ty, tx=tx, tf=tf, tm=tm, tc=tc, cc=cc, one=one, hop=hop_, take=take, prod=prod, out=out, noise=noise.wait)
    for word, *numbers in SCHEDULE:
        if word in ("direct", "edge", "cross", "middle", "one", "hop"):
            numbers = [ORDER[n] for n in numbers]
        actions[word](*numbers)
    for copy, when in sent:
        if when is None:
            copy.wait_send()
        else:
            pl.when(when)(copy.wait_send)
    for copy in outs:
        copy.wait()


def body(covariance, blocks, present, model_noise):
    anywhere = pl.BlockSpec(memory_space=pl.ANY)
    return pl.pallas_call(
        kernel,
        out_shape=jax.ShapeDtypeStruct((768, 768), F32),
        in_specs=[anywhere] * 4,
        out_specs=anywhere,
        scratch_shapes=[
            pltpu.VMEM((CHUNKS, 1792, WIDE), F32),
            pltpu.VMEM((CHUNKS, 256, WIDE), F32),
            pltpu.VMEM((3, 5, 16, 256), F32),
            pltpu.VMEM((CHUNKS, 768 // PARTS, WIDE), F32),
            pltpu.VMEM((16, 3, 5, 16, 256), F32),
            pltpu.VMEM((16, 3, 5, 16, 256), F32),
            pltpu.VMEM((3, 512, 1280), BF16),
            pltpu.VMEM((3, 512, 1280), BF16),
            pltpu.VMEM((1792, 2 * WIDE), BF16),
            pltpu.VMEM((CHUNKS, 768, WIDE), F32),
            pltpu.VMEM((8, 768, WIDE), F32),
            pltpu.VMEM((768, 1792), BF16),
            pltpu.VMEM((768, 1792), BF16),
            pltpu.VMEM((768, 768), F32),
            pltpu.SMEM((48, 5), jnp.int32),
            pltpu.SemaphoreType.DMA((140,)),
            pltpu.SemaphoreType.DMA((140,)),
            pltpu.SemaphoreType.DMA((16,)),
        ],
        compiler_params=pltpu.CompilerParams(collective_id=0, has_side_effects=True, vmem_limit_bytes=60 << 20),
        name="forecast",
    )(covariance, blocks, present, model_noise)


def solution(mesh):
    in_specs = (P("row", "col"), P("col", None, "row", None), P(), P("col", "row"))
    out_specs = P("col", "row")
    return jax.shard_map(body, mesh=mesh, in_specs=in_specs, out_specs=out_specs, check_vma=False)
```

time: 125 us -> 112 us (0.90)
  the two profiles are of different devices: /device:TPU:121 before, /device:TPU:8 now
where the time goes in v2:
time: 112 us
  Pallas kernels  107 us (96%)
  local copies, waits for them, and re-layouts  4.6 us (4%)
    pallas_call x1, Pallas kernels, body(): pl.pallas_call(kernel, out_shape=jax.ShapeDtypeStruct((768, 768), F32), i...  107 us
    unnamed x2, local copies, waits for them, and re-layouts  4.6 us

profile of v2, /device:TPU:8, one launch (start us, length us, event | category | flops | bytes accessed | tf_op | source)
XLA Modules:
  0.0 112.1 jit_solution(15040410987808786565)
XLA Ops:
  0.0 1.4 %copy.5.pres_hbm = s32[48,5]{1,0:T(8,128)} copy(s32[48,5]{0,1:T(8,128)} %param.6) | data formatting | bytes 1920 | tf_op args[2]
  1.4 107.5 %forecast.1 = f32[768,768]{1,0:T(8,128)} custom-call(f32[768,768]{1,0:T(8,128)} %p_hbm.1, f32[3,5,16,256]{3,2,1,0:T(8,128)} %blk_hbm.1, s32[48,5]{1,0:T(8,128)} %copy.5.pres_hbm, f32[768,768]{1,0:T(8,128)} %q_hbm.1), custom_call_target="tpu_custom_call" | custom-call | tf_op jit(solution)/shard_map/forecast/pallas_call | solution.py:363
  108.9 3.2 %copy.7 = f32[768,768]{1,0:T(8,128)} copy(f32[768,768]{1,0:T(8,128)} %forecast.1) | data formatting | bytes 4718592

commit v3 on v2

--- a/solution.py
+++ b/solution.py
@@ -269,15 +269,16 @@
 
     def one(q):
         own[ORDER.index(q)].wait()
-        arrived(f"cross{q}", edge.at[q])
-        arrived(f"middle{q}", edge.at[q])
-
-        @pl.loop(0, 7)
-        def _(t):
+        def narrow(t):
             rows = pl.ds(pl.multiple_of(t * 256, 256), 256)
             high, low = split(win[q, rows])
             win_b[rows, 0:WIDE] = high
             win_b[rows, WIDE : 2 * WIDE] = low
+
+        pl.loop(2, 5)(narrow)
+        arrived(f"cross{q}", edge.at[q])
+        arrived(f"middle{q}", edge.at[q])
+        pl.loop(0, 4)(lambda i: narrow(i + 3 * (i // 2)))
 
         @pl.loop(0, 3)
         def _(i):

time: 112 us -> 112 us (level)
  no operation moved by 1% of the time
where the time goes in v3:
time: 112 us
  Pallas kernels  108 us (96%)
  local copies, waits for them, and re-layouts  4.6 us (4%)
    pallas_call x1, Pallas kernels, body(): pl.pallas_call(kernel, out_shape=jax.ShapeDtypeStruct((768, 768), F32), i...  108 us
    unnamed x2, local copies, waits for them, and re-layouts  4.6 us

profile of v3, /device:TPU:8, one launch (start us, length us, event | category | flops | bytes accessed | tf_op | source)
XLA Modules:
  0.0 112.1 jit_solution(10671745811158807054)
XLA Ops:
  0.0 1.4 %copy.5.pres_hbm = s32[48,5]{1,0:T(8,128)} copy(s32[48,5]{0,1:T(8,128)} %param.6) | data formatting | bytes 1920 | tf_op args[2]
  1.4 107.5 %forecast.1 = f32[768,768]{1,0:T(8,128)} custom-call(f32[768,768]{1,0:T(8,128)} %p_hbm.1, f32[3,5,16,256]{3,2,1,0:T(8,128)} %blk_hbm.1, s32[48,5]{1,0:T(8,128)} %copy.5.pres_hbm, f32[768,768]{1,0:T(8,128)} %q_hbm.1), custom_call_target="tpu_custom_call" | custom-call | tf_op jit(solution)/shard_map/forecast/pallas_call | solution.py:364
  108.9 3.2 %copy.7 = f32[768,768]{1,0:T(8,128)} copy(f32[768,768]{1,0:T(8,128)} %forecast.1) | data formatting | bytes 4718592
